TPU v7x, 256 devices: a whole 4x4x8 slice. The times are simulated.
256 devices in a mesh: grp: 8 (over x, core), row: 32 (over z, y).
Axes of the slice: x: 4, y: 4, z: 8, core: 2. Of those that a mesh axis runs over, the one named last changes fastest.
Arguments:
- placing: int32 [8192], P('grp'), parts along dimension 0, may hold values from 0 to 1023, as said below
- lengths: int32 [512], P('grp'), parts along dimension 0, may hold values from 1 to 48, 1024 in all
- diag_blocks: float32 [8192, 128, 128], P(('grp', 'row')), parts along dimension 0, as said below
- lower_blocks: float32 [8192, 128, 128], P(('grp', 'row')), parts along dimension 0, may hold values from -0.25 to 0.25
- right_side: float32 [8192, 128, 128], P(('grp', 'row')), parts along dimension 0, may hold values from -6 to 6
Outputs:
- solution: float32 [8192, 128, 128], P(('grp', 'row')), parts along dimension 0
- residual: float32 [8192, 128, 128], P(('grp', 'row')), parts along dimension 0
There are 8 independent parts, one for each index of `grp`. A program takes and returns all parts, laid end to end along the dimension named above; each array names one. Nothing has to cross between parts.
Inputs may be any that keep to these rules, and one draw needn't show every extreme that they name: `placing`: A permutation of 0 .. 1023. Device d holds the slots d * 32 .. (d + 1) * 32 - 1, and among them exactly 1 name block rows of each range e * 32 .. (e + 1) * 32 - 1. `lengths`: they sum to 1024. `diag_blocks`: every block is symmetric, and the assembled operator of every system is positive definite.
All inputs are finite; a program needn't handle non-finite values.
Results may differ from a plain program's by a relative error of at most 0.0003.
Values sent between devices are 32-bit elements; how exact they have to be, the bound alone decides.
A program may use at most 128 MiB of HBM per device.

v0:
```python
import jax
import jax.numpy as jnp
from jax import lax
from jax.sharding import PartitionSpec as P

ITERS = 4


HIGHEST = lax.Precision.HIGHEST


def side_by_side(arrays, axis, split_dim, concat_dim, along):
    both = jnp.concatenate(arrays, axis=along)
    whole, at, outs = (
        lax.all_to_all(both, axis, split_axis=split_dim, concat_axis=concat_dim, tiled=True),
        0,
        [],
    )
    for a in arrays:
        outs.append(lax.slice_in_dim(whole, at, at + a.shape[along], axis=along))
        at += a.shape[along]
    return tuple(outs)


def passed_along(x, axis, by):
    count = lax.axis_size(axis)
    pairs = [(i, i + by) for i in range(count) if 0 <= i + by < count]
    return lax.ppermute(x, axis, pairs)


def cut_along(x, dim, count):
    before, after = (x.shape[:dim], x.shape[dim + 1 :])
    return jnp.moveaxis(x.reshape(*before, count, -1, *after), dim, 0)


def summed_on_arrival(x, axis, dim):
    count = lax.axis_size(axis)
    tiles = lax.all_to_all(cut_along(x, dim, count), axis, 0, 0, tiled=True)
    return jnp.sum(tiles, axis=0)


def filled_up(lines, count):
    spare = -lines.shape[0] % count
    if not spare:
        return lines
    return jnp.concatenate([lines, jnp.zeros((spare, *lines.shape[1:]), lines.dtype)])


def laid_out(tiles, dim):
    tiles = jnp.moveaxis(tiles, 0, dim)
    shape = tiles.shape
    return tiles.reshape(*shape[:dim], shape[dim] * shape[dim + 1], *shape[dim + 2 :])


def from_everyone(x, axis):
    count = lax.axis_size(axis)
    return lax.all_to_all(jnp.broadcast_to(x[None], (count, *x.shape)), axis, 0, 0, tiled=True)


def collect(x, axis, dim):
    return laid_out(from_everyone(x, axis), dim)


def nested_sum(x, axes):
    own = summed_on_arrival(filled_up(x, lax.axis_size(axes)), axes, 0)
    whole = collect(own, axes, 0)
    return whole[: len(x)].reshape(x.shape)


def in_one(arrays, axis):
    ravelled, at, outs = (jnp.concatenate([a.reshape(-1) for a in arrays]), 0, [])
    total = nested_sum(ravelled, axis)
    for a in arrays:
        outs.append(total[at : at + a.size].reshape(a.shape))
        at += a.size
    return tuple(outs)


def body(placing, lengths, diag_blocks, lower_blocks, right_side):
    group_size = lax.axis_size("row")
    device = lax.axis_index("row")
    per_dev = diag_blocks.shape[0]
    share_rows = per_dev // group_size
    systems = lengths.shape[0]
    own_slots = lax.dynamic_slice_in_dim(placing, device * per_dev, per_dev)
    by_target = jnp.argsort(own_slots // per_dev, stable=True)
    diag_sorted = diag_blocks[by_target]
    lower_sorted = lower_blocks[by_target]
    rhs_sorted = right_side[by_target]
    slot_table = placing.reshape(group_size, per_dev)
    arranged = jnp.take_along_axis(
        slot_table, jnp.argsort(slot_table // per_dev, axis=1, stable=True), axis=1
    )
    arrived = (
        lax.dynamic_slice_in_dim(arranged, device * share_rows, share_rows, 1).reshape(-1)
        - device * per_dev
    )
    placed = jnp.argsort(arrived)
    diag_in, lower_in, rhs_in = side_by_side(
        (diag_sorted, lower_sorted, rhs_sorted), "row", 0, 0, 1
    )
    diagonal = diag_in[placed]
    rhs_nat = rhs_in[placed]
    seg_ends = jnp.cumsum(lengths)
    starts = seg_ends - lengths
    global_rows = device * per_dev + jnp.arange(per_dev + 1, dtype=jnp.int32)
    is_first = jnp.any(global_rows[:, None] == starts[None, :], axis=1)
    keep_mask = jnp.where(is_first, 0.0, 1.0).astype(jnp.float32)
    segment = jnp.sum((global_rows[:per_dev, None] >= seg_ends[None, :]).astype(jnp.int32), axis=1)
    member = (segment[None, :] == jnp.arange(systems, dtype=jnp.int32)[:, None]).astype(jnp.float32)
    coupling_low = lower_in[placed] * keep_mask[:per_dev, None, None]

    def operate(field):
        center = jnp.einsum("jab,jbk->jak", diagonal, field, precision=HIGHEST)
        before = passed_along(field[-1:], "row", 1)
        shifted_down = jnp.concatenate([before, field[:-1]], axis=0)
        from_below = jnp.einsum("jab,jbk->jak", coupling_low, shifted_down, precision=HIGHEST)
        turned = jnp.einsum("jba,jbk->jak", coupling_low, field, precision=HIGHEST)
        received = passed_along(turned[:1], "row", -1)
        from_above = jnp.concatenate([turned[1:], received], axis=0)
        return center + from_below + from_above

    def per_system(values):
        return jnp.dot(member, jnp.sum(values, axis=1), precision=HIGHEST)

    def spread(coefficient):
        return jnp.dot(member.T, coefficient, precision=HIGHEST)[:, None, :]

    def two_sums(field, image):
        first_local = per_system(field * field)
        second_local = per_system(field * image)
        return in_one((first_local, second_local), "row")

    solution = jnp.zeros_like(rhs_nat)
    residual = rhs_nat
    image = operate(residual)
    norm_now, product = two_sums(residual, image)
    step_size = norm_now / product
    direction = residual
    along_image = image
    for iteration in range(ITERS):
        solution = solution + spread(step_size) * direction
        residual = residual - spread(step_size) * along_image
        if iteration + 1 < ITERS:
            image = operate(residual)
            norm_next, product = two_sums(residual, image)
            beta_ratio = norm_next / norm_now
            step_size = norm_next / (product - beta_ratio * norm_next / step_size)
            direction = residual + spread(beta_ratio) * direction
            along_image = image + spread(beta_ratio) * along_image
            norm_now = norm_next
    return (solution, residual)


def solution(mesh):
    return jax.shard_map(
        body,
        mesh=mesh,
        in_specs=(
            P("grp"),
            P("grp"),
            P(("grp", "row"), None, None),
            P(("grp", "row"), None, None),
            P(("grp", "row"), None, None),
        ),
        out_specs=(P(("grp", "row"), None, None), P(("grp", "row"), None, None)),
        check_vma=False,
    )
```

profile of v0, /device:TPU:4, one launch (start us, length us, event | category | flops | bytes accessed | tf_op | source)
XLA Modules:
  0.0 411.4 jit_solution(16869837305883162232)
XLA Ops:
  1.6 1.6 sort.51
  3.2 2.0 gather_fusion.2
  5.2 3.6 gather_fusion.1
  8.8 3.8 gather_fusion
  12.6 5.6 %pad_maximum_fusion = f32[32,384,128]{2,1,0:T(8,128)} fusion(f32[32,128,128]{2,1,0:T(8,128)S(1)} %copy-done.13, f32[32,128,128]{2,1,0:T(8,128)} %gather_fusion.1, f32[32,128,128]{2,1,0:T(8,128)} %gather_fusion), kind=kLoop, calls=%fused_computation.7 | loop fusion | flops 3145728 | bytes 12582912 | tf_op jit(solution)/shard_map/concatenate | solution.py:13
  18.1 11.7 %all-to-all-start = ((f32[32,384,128]{2,1,0:T(8,128)}), f32[32,384,128]{2,1,0:T(8,128)}, u32[]{:S(2)}, u32[]{:S(2)}) async-start(f32[32,384,128]{2,1,0:T(8,128)} %pad_maximum_fusion), calls=%async_computation | async-start | bytes 12582912 | tf_op jit(solution)/shard_map/all_to_all | solution.py:15
  31.0 7.1 %gather_fusion.6 = s32[1024]{0:T(1024)S(1)} fusion(s32[32,32]{1,0:T(8,128)S(1)} %reshape.179, s32[1024]{0:T(1024)S(1)} %reshape.237), kind=kCustom, calls=%fused_computation.6 | custom fusion | bytes 16384 | tf_op jit(solution)/shard_map/jit(take_along_axis)/gather | solution.py:91
  38.7 1.6 sort.53
  40.7 127.4 %all-to-all-done = f32[32,384,128]{2,1,0:T(8,128)} async-done(((f32[32,384,128]{2,1,0:T(8,128)}), f32[32,384,128]{2,1,0:T(8,128)}, u32[]{:S(2)}, u32[]{:S(2)}) %all-to-all-start) | async-done | bytes 6291488 | tf_op jit(solution)/shard_map/all_to_all | solution.py:15
  168.1 5.7 %fusion.89 = (f32[32,128,128]{2,1,0:T(8,128)S(1)}, f32[32,128,128]{2,1,0:T(8,128)}, f32[32,128,128]{2,1,0:T(8,128)}) fusion(f32[32,384,128]{2,1,0:T(8,128)} %all-to-all-done), kind=kLoop, calls=%fused_computation.136 | loop fusion | bytes 12582912 | tf_op jit(solution)/shard_map/slice | solution.py:20
  173.7 2.0 gather_fusion.4
  175.7 2.3 gather_fusion.5
  178.0 3.6 gather_fusion.3
  182.4 8.8 %collective-permute-start = (f32[1,128,128]{2,1,0:T(8,128)S(1)}, f32[1,128,128]{2,1,0:T(8,128)S(1)}, u32[]{:S(2)}, u32[]{:S(2)}) collective-permute-start(f32[1,128,128]{2,1,0:T(8,128)S(1)} %slice.149), channel_id=1, source_target_pairs={{0,1},{1,2},{2,3},{3,4},{4,5},{5,6},{6,7},{7,8},{8,9},{9,10},{10,1... | collective-permute-start | bytes 196616 | tf_op jit(solution)/shard_map/ppermute | solution.py:28
  191.2 5.3 %fusion.27 = f32[32,128,128]{2,1,0:T(8,128)S(1)} fusion(f32[32,128,128]{2,1,0:T(8,128)} %gather_fusion.3, f32[32,128,128]{2,1,0:T(8,128)S(1)} %gather_fusion.5, f32[32]{0:T(128)S(1)} %bitcast.56), kind=kOutput, calls=%fused_computation.52 | convolution fusion | flops 805830656 | bytes 6291584 | tf_op jit(solution)/shard_map/jba,jbk->jak/dot_general | solution.py:118
  196.5 1.6 collective-permute-start.1
  198.1 2.3 fusion.94
  200.6 2.1 collective-permute-done.1
  202.7 4.3 %multiply_reduce_fusion.7 = (f32[32,128]{1,0:T(8,128)S(1)}, f32[32,128]{1,0:T(8,128)S(1)}, f32[32,128,128]{2,1,0:T(8,128)}) fusion(f32[32,128,128]{2,1,0:T(8,128)S(1)} %copy-done.3, f32[1,128,128]{2,1,0:T(8,128)S(1)} %collective-permute-done.1, f32[31,128,128]{2,1,0:T(8,128)S(1)} %slice.151, f32[32,128,128]{2,1,0:T(8,128)S(1)} %fusion.94, ...), kind=kOutput, calls=%fused_computation.42 | convolution fusion | flops 810016768 | bytes 12615808 | tf_op jit(solution)/shard_map/jab,jbk->jak/dot_general | solution.py:117
  207.4 20.8 %all_to_all.65 = f32[32,1,512]{2,1,0:T(1,128)S(1)} all-to-all(f32[32,1,512]{2,1,0:T(1,128)S(1)} %all_to_all.44), channel_id=1, replica_groups=mesh['grp'=8,'row'=32] {'row'}, dimensions={0} | all-to-all | bytes 131072 | tf_op jit(solution)/shard_map/all_to_all | solution.py:38
  228.3 13.1 %all_to_all.66 = f32[32,1,512]{2,1,0:T(1,128)S(1)} all-to-all(f32[32,1,512]{2,1,0:T(1,128)S(1)} %broadcast_in_dim.29), channel_id=1, replica_groups=mesh['grp'=8,'row'=32] {'row'}, dimensions={0} | all-to-all | bytes 131072 | tf_op jit(solution)/shard_map/all_to_all | solution.py:57
  241.5 2.6 multiply_subtract_fusion.3
  244.2 3.7 fusion.24
  247.9 2.4 collective-permute-start.2
  250.4 1.8 collective-permute-start.3
  252.2 2.3 fusion.95
  254.7 1.8 collective-permute-done.3
  256.5 5.5 %multiply_reduce_fusion.5 = (f32[32,128]{1,0:T(8,128)S(1)}, f32[32,128]{1,0:T(8,128)S(1)}, f32[32,128,128]{2,1,0:T(8,128)}) fusion(f32[32,128,128]{2,1,0:T(8,128)} %copy-done.4, f32[1,128,128]{2,1,0:T(8,128)S(1)} %collective-permute-done.3, f32[31,128,128]{2,1,0:T(8,128)S(1)} %slice.157, f32[32,128,128]{2,1,0:T(8,128)S(1)} %fusion.95, ...), kind=kOutput, calls=%fused_computation.39 | convolution fusion | flops 810016768 | bytes 12615808 | tf_op jit(solution)/shard_map/jab,jbk->jak/dot_general | solution.py:117
  262.4 17.9 %all_to_all.67 = f32[32,1,512]{2,1,0:T(1,128)S(1)} all-to-all(f32[32,1,512]{2,1,0:T(1,128)S(1)} %all_to_all.47), channel_id=1, replica_groups=mesh['grp'=8,'row'=32] {'row'}, dimensions={0} | all-to-all | bytes 131072 | tf_op jit(solution)/shard_map/all_to_all | solution.py:38
  280.4 13.1 %all_to_all.68 = f32[32,1,512]{2,1,0:T(1,128)S(1)} all-to-all(f32[32,1,512]{2,1,0:T(1,128)S(1)} %broadcast_in_dim.30), channel_id=1, replica_groups=mesh['grp'=8,'row'=32] {'row'}, dimensions={0} | all-to-all | bytes 131072 | tf_op jit(solution)/shard_map/all_to_all | solution.py:57
  293.9 3.6 multiply_subtract_fusion.2
  297.5 3.7 fusion.21
  301.2 2.4 collective-permute-start.4
  305.1 2.3 fusion.96
  307.6 2.2 collective-permute-done.5
  309.8 5.5 %multiply_reduce_fusion.3 = (f32[32,128]{1,0:T(8,128)S(1)}, f32[32,128]{1,0:T(8,128)S(1)}, f32[32,128,128]{2,1,0:T(8,128)}) fusion(f32[32,128,128]{2,1,0:T(8,128)} %copy-done.5, f32[1,128,128]{2,1,0:T(8,128)S(1)} %collective-permute-done.5, f32[31,128,128]{2,1,0:T(8,128)S(1)} %slice.163, f32[32,128,128]{2,1,0:T(8,128)S(1)} %fusion.96, ...), kind=kOutput, calls=%fused_computation.35 | convolution fusion | flops 810016768 | bytes 12615808 | tf_op jit(solution)/shard_map/jab,jbk->jak/dot_general | solution.py:117
  315.7 17.9 %all_to_all.69 = f32[32,1,512]{2,1,0:T(1,128)S(1)} all-to-all(f32[32,1,512]{2,1,0:T(1,128)S(1)} %all_to_all.50), channel_id=1, replica_groups=mesh['grp'=8,'row'=32] {'row'}, dimensions={0} | all-to-all | bytes 131072 | tf_op jit(solution)/shard_map/all_to_all | solution.py:38
  333.7 13.1 %all_to_all.70 = f32[32,1,512]{2,1,0:T(1,128)S(1)} all-to-all(f32[32,1,512]{2,1,0:T(1,128)S(1)} %broadcast_in_dim.31), channel_id=1, replica_groups=mesh['grp'=8,'row'=32] {'row'}, dimensions={0} | all-to-all | bytes 131072 | tf_op jit(solution)/shard_map/all_to_all | solution.py:57
  347.2 6.0 %multiply_subtract_fusion.1 = (f32[32,128,128]{2,1,0:T(8,128)S(1)}, f32[32,128,128]{2,1,0:T(8,128)}) fusion(f32[32,128,128]{2,1,0:T(8,128)} %copy-done.5, f32[32,128]{1,0:T(8,128)S(1)} %fusion.51, f32[32,128,128]{2,1,0:T(8,128)} %get-tuple-element.33, f32[32,128,128]{2,1,0:T(8,128)} %get-tuple-element.32, f32[32,128,128]{2,1,0:T(8,128)} %get-tuple-element.31, ...), kind=kLoop, calls=%fused_computation.32 | loop fusion | flops 3145728 | bytes 12632064 | tf_op jit(solution)/shard_map/sub | solution.py:143
  353.3 2.4 collective-permute-start.6
  355.7 3.7 fusion.18
  359.7 1.8 collective-permute-start.7
  361.5 2.4 fusion.12
  363.9 2.2 collective-permute-done.7
  366.2 4.2 %multiply_reduce_fusion.1 = (f32[32,128]{1,0:T(8,128)S(1)}, f32[32,128]{1,0:T(8,128)S(1)}, f32[32,128,128]{2,1,0:T(8,128)}) fusion(f32[32,128,128]{2,1,0:T(8,128)S(1)} %get-tuple-element.16, f32[1,128,128]{2,1,0:T(8,128)S(1)} %collective-permute-done.7, f32[31,128,128]{2,1,0:T(8,128)S(1)} %slice.169, f32[32,128,128]{2,1,0:T(8,128)S(1)} %fusion.12, ...), kind=kOutput, calls=%fused_computation.31 | convolution fusion | flops 808968192 | bytes 10518528 | tf_op jit(solution)/shard_map/jab,jbk->jak/dot_general | solution.py:114
  370.7 17.9 %all_to_all.71 = f32[32,1,512]{2,1,0:T(1,128)S(1)} all-to-all(f32[32,1,512]{2,1,0:T(1,128)S(1)} %all_to_all.53), channel_id=1, replica_groups=mesh['grp'=8,'row'=32] {'row'}, dimensions={0} | all-to-all | bytes 131072 | tf_op jit(solution)/shard_map/all_to_all | solution.py:38
  388.8 13.1 %all_to_all.72 = f32[32,1,512]{2,1,0:T(1,128)S(1)} all-to-all(f32[32,1,512]{2,1,0:T(1,128)S(1)} %broadcast_in_dim.32), channel_id=1, replica_groups=mesh['grp'=8,'row'=32] {'row'}, dimensions={0} | all-to-all | bytes 131072 | tf_op jit(solution)/shard_map/all_to_all | solution.py:57
  402.3 8.9 %multiply_subtract_fusion = (f32[32,128,128]{2,1,0:T(8,128)}, f32[32,128,128]{2,1,0:T(8,128)}) fusion(f32[32,128,128]{2,1,0:T(8,128)} %copy-done.10, f32[32,128,128]{2,1,0:T(8,128)} %get-tuple-element.17, f32[1,128,128]{2,1,0:T(8,128)S(1)} %collective-permute-done.7, f32[31,128,128]{2,1,0:T(8,128)} %copy-done.12, f32[32,128,128]{2,1,0:T(8,128)} %get-tuple-element.34, ...), kind=kLoop, calls=%fused_computation.28 | loop fusion | flops 10485760 | bytes 21086208 | tf_op jit(solution)/shard_map/sub | solution.py:143
  (128 shorter events, 9.4 us)
Async XLA Ops:
  0.6 2.6 copy-start
  8.8 3.8 copy-start.13
  18.1 11.7 %copy-start.14 = (s32[1024]{0:T(1024)S(1)}, s32[1024]{0:T(1024)}, u32[]{:S(2)}) copy-start(s32[1024]{0:T(1024)} %param.5) | copy-start | bytes 12292
  18.1 149.9 %all-to-all-start = ((f32[32,384,128]{2,1,0:T(8,128)}), f32[32,384,128]{2,1,0:T(8,128)}, u32[]{:S(2)}, u32[]{:S(2)}) async-start(f32[32,384,128]{2,1,0:T(8,128)} %pad_maximum_fusion), calls=%async_computation | async-start | bytes 12582912 | tf_op jit(solution)/shard_map/all_to_all | solution.py:15
  31.0 7.3 %copy-start.15 = (s32[64]{0:T(128)S(1)}, s32[64]{0:T(128)}, u32[]{:S(2)}) copy-start(s32[64]{0:T(128)} %param.6) | copy-start | bytes 772
  182.4 18.2 %collective-permute-start = (f32[1,128,128]{2,1,0:T(8,128)S(1)}, f32[1,128,128]{2,1,0:T(8,128)S(1)}, u32[]{:S(2)}, u32[]{:S(2)}) collective-permute-start(f32[1,128,128]{2,1,0:T(8,128)S(1)} %slice.149), channel_id=1, source_target_pairs={{0,1},{1,2},{2,3},{3,4},{4,5},{5,6},{6,7},{7,8},{8,9},{9,10},{10,1... | collective-permute-start | bytes 196616 | tf_op jit(solution)/shard_map/ppermute | solution.py:28
  191.2 6.9 %copy-start.2 = (f32[32,128,128]{2,1,0:T(8,128)S(1)}, f32[32,128,128]{2,1,0:T(8,128)}, u32[]{:S(2)}) copy-start(f32[32,128,128]{2,1,0:T(8,128)} %gather_fusion.3) | copy-start | bytes 6291460
  191.2 6.9 %copy-start.6 = (f32[32,128,128]{2,1,0:T(8,128)S(1)}, f32[32,128,128]{2,1,0:T(8,128)}, u32[]{:S(2)}) copy-start(f32[32,128,128]{2,1,0:T(8,128)} %gather_fusion.4) | copy-start | bytes 6291460
  196.5 6.2 %collective-permute-start.1 = (f32[1,128,128]{2,1,0:T(8,128)S(1)}, f32[1,128,128]{2,1,0:T(8,128)S(1)}, u32[]{:S(2)}, u32[]{:S(2)}) collective-permute-start(f32[1,128,128]{2,1,0:T(8,128)S(1)} %slice.152), channel_id=1, source_target_pairs={{1,0},{2,1},{3,2},{4,3},{5,4},{6,5},{7,6},{8,7},{9,8},{10,9},{11,1... | collective-permute-start | bytes 196616 | tf_op jit(solution)/shard_map/ppermute | solution.py:28
  200.5 2.2 copy-start.3
  200.5 2.2 slice-start
  244.2 10.3 %copy-start.4 = (f32[32,128,128]{2,1,0:T(8,128)}, f32[32,128,128]{2,1,0:T(8,128)S(1)}, u32[]{:S(2)}) copy-start(f32[32,128,128]{2,1,0:T(8,128)S(1)} %multiply_subtract_fusion.3) | copy-start | bytes 6291460
  244.2 8.0 %copy-start.7 = (f32[32,128,128]{2,1,0:T(8,128)S(1)}, f32[32,128,128]{2,1,0:T(8,128)}, u32[]{:S(2)}) copy-start(f32[32,128,128]{2,1,0:T(8,128)} %gather_fusion.4) | copy-start | bytes 6291460
  247.9 6.8 %collective-permute-start.2 = (f32[1,128,128]{2,1,0:T(8,128)S(1)}, f32[1,128,128]{2,1,0:T(8,128)S(1)}, u32[]{:S(2)}, u32[]{:S(2)}) collective-permute-start(f32[1,128,128]{2,1,0:T(8,128)S(1)} %slice.155), channel_id=1, source_target_pairs={{0,1},{1,2},{2,3},{3,4},{4,5},{5,6},{6,7},{7,8},{8,9},{9,10},{10,1... | collective-permute-start | bytes 196616 | tf_op jit(solution)/shard_map/ppermute | solution.py:28
  250.4 6.2 %collective-permute-start.3 = (f32[1,128,128]{2,1,0:T(8,128)S(1)}, f32[1,128,128]{2,1,0:T(8,128)S(1)}, u32[]{:S(2)}, u32[]{:S(2)}) collective-permute-start(f32[1,128,128]{2,1,0:T(8,128)S(1)} %slice.158), channel_id=1, source_target_pairs={{1,0},{2,1},{3,2},{4,3},{5,4},{6,5},{7,6},{8,7},{9,8},{10,9},{11,1... | collective-permute-start | bytes 196616 | tf_op jit(solution)/shard_map/ppermute | solution.py:28
  254.5 2.0 slice-start.1
  297.5 10.0 %copy-start.5 = (f32[32,128,128]{2,1,0:T(8,128)}, f32[32,128,128]{2,1,0:T(8,128)S(1)}, u32[]{:S(2)}) copy-start(f32[32,128,128]{2,1,0:T(8,128)S(1)} %multiply_subtract_fusion.2) | copy-start | bytes 6291460
  297.5 7.6 %copy-start.8 = (f32[32,128,128]{2,1,0:T(8,128)S(1)}, f32[32,128,128]{2,1,0:T(8,128)}, u32[]{:S(2)}) copy-start(f32[32,128,128]{2,1,0:T(8,128)} %gather_fusion.4) | copy-start | bytes 6291460
  301.2 6.4 %collective-permute-start.4 = (f32[1,128,128]{2,1,0:T(8,128)S(1)}, f32[1,128,128]{2,1,0:T(8,128)S(1)}, u32[]{:S(2)}, u32[]{:S(2)}) collective-permute-start(f32[1,128,128]{2,1,0:T(8,128)S(1)} %slice.161), channel_id=1, source_target_pairs={{0,1},{1,2},{2,3},{3,4},{4,5},{5,6},{6,7},{7,8},{8,9},{9,10},{10,1... | collective-permute-start | bytes 196616 | tf_op jit(solution)/shard_map/ppermute | solution.py:28
  303.7 6.2 %collective-permute-start.5 = (f32[1,128,128]{2,1,0:T(8,128)S(1)}, f32[1,128,128]{2,1,0:T(8,128)S(1)}, u32[]{:S(2)}, u32[]{:S(2)}) collective-permute-start(f32[1,128,128]{2,1,0:T(8,128)S(1)} %slice.164), channel_id=1, source_target_pairs={{1,0},{2,1},{3,2},{4,3},{5,4},{6,5},{7,6},{8,7},{9,8},{10,9},{11,1... | collective-permute-start | bytes 196616 | tf_op jit(solution)/shard_map/ppermute | solution.py:28
  307.5 2.4 slice-start.2
  353.3 12.9 %copy-start.10 = (f32[32,128,128]{2,1,0:T(8,128)}, f32[32,128,128]{2,1,0:T(8,128)S(1)}, u32[]{:S(2)}) copy-start(f32[32,128,128]{2,1,0:T(8,128)S(1)} %get-tuple-element.16) | copy-start | bytes 6291460
  353.3 8.2 %collective-permute-start.6 = (f32[1,128,128]{2,1,0:T(8,128)S(1)}, f32[1,128,128]{2,1,0:T(8,128)S(1)}, u32[]{:S(2)}, u32[]{:S(2)}) collective-permute-start(f32[1,128,128]{2,1,0:T(8,128)S(1)} %slice.167), channel_id=1, source_target_pairs={{0,1},{1,2},{2,3},{3,4},{4,5},{5,6},{6,7},{7,8},{8,9},{9,10},{10,1... | collective-permute-start | bytes 196616 | tf_op jit(solution)/shard_map/ppermute | solution.py:28
  359.7 6.4 %copy-start.12 = (f32[31,128,128]{2,1,0:T(8,128)}, f32[31,128,128]{2,1,0:T(8,128)S(1)}, u32[]{:S(2)}) copy-start(f32[31,128,128]{2,1,0:T(8,128)S(1)} %slice.169) | copy-start | bytes 6094852
  359.7 6.4 %copy-start.9 = (f32[32,128,128]{2,1,0:T(8,128)S(1)}, f32[32,128,128]{2,1,0:T(8,128)}, u32[]{:S(2)}) copy-start(f32[32,128,128]{2,1,0:T(8,128)} %gather_fusion.4) | copy-start | bytes 6291460
  359.7 6.4 %collective-permute-start.7 = (f32[1,128,128]{2,1,0:T(8,128)S(1)}, f32[1,128,128]{2,1,0:T(8,128)S(1)}, u32[]{:S(2)}, u32[]{:S(2)}) collective-permute-start(f32[1,128,128]{2,1,0:T(8,128)S(1)} %slice.170), channel_id=1, source_target_pairs={{1,0},{2,1},{3,2},{4,3},{5,4},{6,5},{7,6},{8,7},{9,8},{10,9},{11,1... | collective-permute-start | bytes 196616 | tf_op jit(solution)/shard_map/ppermute | solution.py:28
  363.9 6.4 %copy-start.11 = (f32[32,128,128]{2,1,0:T(8,128)}, f32[32,128,128]{2,1,0:T(8,128)S(1)}, u32[]{:S(2)}) copy-start(f32[32,128,128]{2,1,0:T(8,128)S(1)} %fusion.12) | copy-start | bytes 6291460
  402.3 8.9 %copy-start.1 = (f32[32,128,128]{2,1,0:T(8,128)S(1)}, f32[32,128,128]{2,1,0:T(8,128)}, u32[]{:S(2)}) copy-start(f32[32,128,128]{2,1,0:T(8,128)} %param.9) | copy-start | bytes 6291460
where the time goes:
time: 418 us; the launch traced here: 411 us
  waiting for transfers between devices  136 us (33%)
  blocking collectives  127 us (30%)
  matrix products  47.6 us (11%)
  starting transfers between devices  34.4 us (8%)
  local copies, waits for them, and re-layouts  32.6 us (8%)
  other arithmetic  32.6 us (8%)
    all_to_all x1, waiting for transfers between devices, side_by_side(): lax.all_to_all(both, axis, split_axis=split_dim, concat_axis=concat_dim,...  127 us
    all_to_all x4, blocking collectives, summed_on_arrival(): tiles = lax.all_to_all(cut_along(x, dim, count), axis, 0, 0, tiled=True)  74.5 us
    all_to_all x4, blocking collectives, from_everyone(): lax.all_to_all(jnp.broadcast_to(x[None], (count, *x.shape)), axis, 0, 0,...  52.3 us
    ppermute x8, starting transfers between devices, passed_along(): return lax.ppermute(x, axis, pairs)  22.7 us
    sub x4, other arithmetic, body(): residual = residual - spread(step_size) * along_image  21.2 us
    dot_general x4, matrix products, operate(): jnp.einsum('jab,jbk->jak', coupling_low, shifted_down, precision=HIGHEST)  17.6 us
    dot_general x4, matrix products, operate(): turned = jnp.einsum('jba,jbk->jak', coupling_low, field, precision=HIGHEST)  16.3 us
    all_to_all x1, starting transfers between devices, side_by_side(): lax.all_to_all(both, axis, split_axis=split_dim, concat_axis=concat_dim,...  11.7 us
  transfers between devices with their start and end apart: 9, of which 5 were waited for; matrix products, arithmetic and copies ran while one was open for 7% of the time, Pallas kernels for 0%

commit v1 on v0

v1 whole, which is shorter than its diff:
```python
import functools

import jax
import jax.numpy as jnp
from jax import lax
from jax.experimental import pallas as pl
from jax.experimental.pallas import tpu as pltpu
from jax.sharding import PartitionSpec as P

ITERS = 4
NZ, NY = 8, 4
N = NZ * NY
BPD = 32
B = 128
H = B // 2
SYSTEMS = 64
DROWS = H + 8
CHUNKS = 4
F32, BF16 = jnp.float32, jnp.bfloat16
HIGHEST = lax.Precision.HIGHEST
MESH = pl.DeviceIdType.MESH


def iota(shape, dim):
    return lax.broadcasted_iota(jnp.int32, shape, dim)


def halves(v):
    hi = v.astype(BF16)
    return hi, (v - hi.astype(F32)).astype(BF16)


def side(v):
    return jnp.concatenate(halves(v), axis=1)


def times(left, right):
    out = jnp.dot(left, jnp.concatenate([right, right], axis=0), preferred_element_type=F32)
    return out[:, :B] + out[:, B:]


def triangle_of(block):
    top, bottom = block[:H], block[H:]
    row, lane = iota((H, B), 0), iota((H, B), 1)
    turned = pltpu.roll(bottom, H, 1)
    body = jnp.where((lane < H) & (row > lane), turned, top)
    diagonal = jnp.sum(jnp.where(row + H == lane, bottom, 0.0), axis=0, keepdims=True)
    return body, diagonal


def whole_of(body, diagonal):
    row, lane = iota((H, B), 0), iota((H, B), 1)
    low = jnp.where(row + H == lane, diagonal, pltpu.roll(body, H, 1))
    known = jnp.concatenate([body, low], axis=0)
    row, lane = iota((B, B), 0), iota((B, B), 1)
    top = row < H
    mask = (top & (lane >= row)) | (~top & (lane >= H) & (lane <= row))
    return jnp.where(mask, known, known.T)


def kernel(
    table, lengths, rhs_hbm, diag_hbm, low_hbm, x_hbm, r_hbm,
    st_f, st_d, st_l, sd_f, sd_d, sd_l, rc_f, rc_d, rc_l,
    w_d, w_t, w_l, x, r, p, s, im, rw, ss_rows, keep, near, alpha, beta,
    halo_p, halo_t, turned, part, parts, x_out, r_out,
    in_sem, a2a_send, a2a_recv, halo_send, halo_recv, part_send, part_recv, out_sem,
):
    me = lax.axis_index("row")
    z, y = me // NY, me % NY

    def away(i, way):
        dy, k = i // NZ, i % NZ
        dz = ((k + 1) // 2) * (2 * (k % 2) - 1)
        return ((z + way * dz + NZ) % NZ) * NY + (y + way * dy + NY) % NY

    def slot_of(t):
        return table[t]

    def row_of(d):
        return table[N + d]

    def src_of(l):
        return table[2 * N + l]

    barrier = pltpu.get_barrier_semaphore()

    def greet(i, carry):
        pl.semaphore_signal(barrier, 1, device_id={"row": away(i, 1)}, device_id_type=MESH)
        return carry

    def sent(phase, i, src, dst):
        t = away(i, 1)
        return pltpu.make_async_remote_copy(
            src.at[t], dst.at[me], a2a_send.at[phase, i], a2a_recv.at[phase, i],
            device_id={"row": t}, device_id_type=MESH,
        )

    def arriving(phase, i, src, dst):
        d = away(i, -1)
        return pltpu.make_async_remote_copy(
            src.at[d], dst.at[d], a2a_send.at[phase, i], a2a_recv.at[phase, i],
            device_id={"row": d}, device_id_type=MESH,
        )

    phases = ((sd_l, rc_l), (sd_d, rc_d), (sd_f, rc_f))
    owns = [
        pltpu.make_async_copy(src.at[me], dst.at[me], in_sem.at[3 + k]) for k, (src, dst) in enumerate(phases)
    ]

    def send_all(phase):
        src, dst = phases[phase]

        def start(i, carry):
            sent(phase, i, src, dst).start()
            return carry

        lax.fori_loop(1, N, start, 0)
        owns[phase].start()

    def receive_all(phase):
        src, dst = phases[phase]

        def wait(i, carry):
            arriving(phase, i, src, dst).wait_recv()
            return carry

        lax.fori_loop(1, N, wait, 0)
        owns[phase].wait()

    loads = [
        pltpu.make_async_copy(src, dst, in_sem.at[k])
        for k, (src, dst) in enumerate(((low_hbm, st_l), (diag_hbm, st_d), (rhs_hbm, st_f)))
    ]
    lax.fori_loop(1, N, greet, 0)
    for load in loads:
        load.start()
    loads[0].wait()

    def gather_l(t, carry):
        sd_l[t] = st_l[slot_of(t)]
        return carry

    def gather_d(t, carry):
        body, diagonal = triangle_of(st_d[slot_of(t)])
        sd_d[t, 0:H] = body
        sd_d[t, H:DROWS] = jnp.broadcast_to(diagonal, (8, B))
        return carry

    def gather_f(t, carry):
        sd_f[t] = st_f[slot_of(t)]
        return carry

    lax.fori_loop(0, N, gather_l, 0)
    pl.semaphore_wait(barrier, N - 1)
    send_all(0)
    loads[1].wait()
    lax.fori_loop(0, N, gather_d, 0)
    send_all(1)
    loads[2].wait()
    lax.fori_loop(0, N, gather_f, 0)
    send_all(2)

    base = me * BPD
    rows = iota((BPD, B), 0) + base
    lane = iota((BPD, B), 1)
    eighths = base + iota((BPD, 8 * BPD), 1) // 8
    cols = jnp.full((BPD, B), -1, jnp.int32)
    for k, j in enumerate((base - 1, base - BPD - 1, base + BPD, base + 2 * BPD)):
        cols = jnp.where(lane == k, j, cols)

    def count(q, carry):
        end, a, b, c, e = carry
        end = end + lengths[q]
        one = lambda m: jnp.where(m, 1, 0)
        return (
            end, a + one(rows >= end), b + one(cols >= end), c + one(rows - 1 >= end), e + one(eighths >= end),
        )

    zero = jnp.zeros((BPD, B), jnp.int32)
    _, seg, seg_cols, seg_before, seg_eighths = lax.fori_loop(
        0, SYSTEMS, count, (jnp.int32(0), zero, zero, zero, jnp.zeros((BPD, 8 * BPD), jnp.int32))
    )
    keep[...] = jnp.where((seg != seg_before) | (rows == 0), 0.0, 1.0)
    same = jnp.where((seg == seg_cols) & (cols >= 0), 1.0, 0.0).astype(F32)
    for k in range(4):
        near[k] = jnp.broadcast_to(same[:, k : k + 1], (BPD, B))
    same_here = jnp.where(jnp.concatenate([seg, seg], axis=1) == seg_eighths, 1.0, 0.0).astype(F32)

    receive_all(0)

    def open_l(d, carry):
        v = rc_l[d] * keep[pl.ds(row_of(d), 1)]
        w_l[d] = side(v)
        w_t[d] = side(v.T)
        return carry

    lax.fori_loop(0, N, open_l, 0)
    receive_all(1)

    def open_d(d, carry):
        w_d[d] = side(whole_of(rc_d[d, 0:H], rc_d[d, H : H + 1]))
        return carry

    lax.fori_loop(0, N, open_d, 0)
    receive_all(2)

    def settle(l, carry):
        v = rc_f[src_of(l)]
        r[l] = v
        rw[l] = side(v)
        return carry

    lax.fori_loop(0, BPD, settle, 0)

    def shift(by):
        return (me + by + N) % N

    def remote(src, dst, send, recv, by):
        return pltpu.make_async_remote_copy(
            src, dst, send, recv, device_id={"row": shift(by)}, device_id_type=MESH
        )

    def multiply(it):
        down = remote(r.at[BPD - 1], halo_p.at[it], halo_send.at[it, 0], halo_recv.at[it, 0], 1)
        up = remote(turned.at[it], halo_t.at[it], halo_send.at[it, 1], halo_recv.at[it, 1], -1)
        down.start()

        def products(j, last=False):
            here = src_of(j)
            mats = [w_t[here], w_d[here]]
            if not last:
                mats.append(w_l[src_of(j + 1)])
            out = times(jnp.concatenate(mats, axis=0), rw[j])
            return [out[k * B : (k + 1) * B] for k in range(len(mats))]

        t, c, b = products(0)
        turned[it] = t
        up.start()
        im[0] = c
        im[1] = b

        def step(j, carry):
            t, c, b = products(j)
            im[j - 1] = im[j - 1] + t
            im[j] = im[j] + c
            im[j + 1] = b
            return carry

        lax.fori_loop(1, BPD - 1, step, 0)
        t, c = products(BPD - 1, last=True)
        im[BPD - 2] = im[BPD - 2] + t
        im[BPD - 1] = im[BPD - 1] + c
        down.wait_recv()
        im[0] = im[0] + times(w_l[src_of(0)], side(halo_p[it]))
        up.wait_recv()
        im[BPD - 1] = im[BPD - 1] + halo_t[it]
        down.wait_send()
        up.wait_send()

    def two_sums(it):
        def row_sums(l, carry):
            v = r[l]
            at = pl.ds(pl.multiple_of(8 * l, 8), 8)
            ss_rows[at, 0:B] = jnp.sum((v * v).reshape(B // 8, 8, B), axis=0)
            ss_rows[at, B : 2 * B] = jnp.sum((v * im[l]).reshape(B // 8, 8, B), axis=0)
            return carry

        lax.fori_loop(0, BPD, row_sums, 0)
        local = jnp.dot(same_here, ss_rows[...], precision=HIGHEST, preferred_element_type=F32)
        for k, row in enumerate((0, BPD - 1)):
            part[it, k, 0:1] = local[row : row + 1, :B]
            part[it, k, 1:2] = local[row : row + 1, B:]
        copies = [
            remote(part.at[it, k], parts.at[it, q], part_send.at[it, q], part_recv.at[it, q], by)
            for q, (k, by) in enumerate(((1, 1), (1, 2), (0, -1), (0, -2)))
        ]
        for copy in copies:
            copy.start()
        first, second = local[:, :B], local[:, B:]
        for copy in copies:
            copy.wait_recv()
            copy.wait_send()
        for q in range(4):
            first = first + near[q] * parts[it, q, 0:1]
            second = second + near[q] * parts[it, q, 1:2]
        return first, second

    for it in range(ITERS):
        multiply(it)
        norm, product = two_sums(it)
        if it == 0:
            step_size = norm / product
        else:
            ratio = norm / norm_before
            step_size = norm / (product - ratio * norm / step_size)
            beta[...] = ratio
        alpha[...] = step_size
        norm_before = norm

        def update(l, carry, it=it):
            a = alpha[pl.ds(l, 1)]
            res, image = r[l], im[l]
            if it == 0:
                direction, along = res, image
                x[l] = a * direction
            else:
                b = beta[pl.ds(l, 1)]
                direction = res + b * p[l]
                along = image + b * s[l]
                x[l] = x[l] + a * direction
            res = res - a * along
            r[l] = res
            p[l] = direction
            s[l] = along
            rw[l] = side(res)
            return carry

        if it + 1 < ITERS:
            lax.fori_loop(0, BPD, update, 0)

    outs = []
    span = BPD // CHUNKS
    for c in range(CHUNKS):
        def finish(q, carry, c=c):
            l = c * span + q
            a = alpha[pl.ds(l, 1)]
            res, image = r[l], im[l]
            b = beta[pl.ds(l, 1)]
            x_out[c][q] = x[l] + a * (res + b * p[l])
            r_out[c][q] = res - a * (image + b * s[l])
            return carry

        lax.fori_loop(0, span, finish, 0)
        for k, (src, dst) in enumerate(((x_out, x_hbm), (r_out, r_hbm))):
            outs.append(pltpu.make_async_copy(src[c], dst.at[pl.ds(c * span, span)], out_sem.at[c, k]))
            outs[-1].start()

    def drained(i, carry):
        for phase, (src, dst) in enumerate(phases):
            sent(phase, i, src, dst).wait_send()
        return carry

    lax.fori_loop(1, N, drained, 0)
    for out in outs:
        out.wait()


def body(placing, lengths, diag_blocks, lower_blocks, right_side):
    me = lax.axis_index("row")
    slots = placing.reshape(N, BPD)
    owner, local = slots // BPD, slots % BPD
    index = jnp.arange(BPD, dtype=jnp.int32)
    own = lax.dynamic_slice_in_dim(owner, me, 1, 0)
    slot_of = jnp.sum(jnp.where(own == index[:, None], index[None, :], 0), axis=1)
    row_of = jnp.sum(jnp.where(owner == me, local, 0), axis=1)
    src_of = jnp.sum(
        jnp.where((owner == me) & (local == index[:, None, None]), index[None, :, None], 0), axis=(1, 2)
    )
    table = jnp.concatenate([slot_of, row_of, src_of]).astype(jnp.int32)
    field = jax.ShapeDtypeStruct((BPD, B, B), F32)
    smem, hbm = pl.BlockSpec(memory_space=pltpu.SMEM), pl.BlockSpec(memory_space=pl.ANY)
    blocks = pltpu.VMEM((BPD, B, B), F32)
    packed = pltpu.VMEM((BPD, DROWS, B), F32)
    pairs = pltpu.VMEM((BPD, B, 2 * B), BF16)
    lines = pltpu.VMEM((BPD, B), F32)
    halo = pltpu.VMEM((ITERS, B, B), F32)
    dma = pltpu.SemaphoreType.DMA
    return pl.pallas_call(
        kernel,
        out_shape=(field, field),
        in_specs=[smem, smem, hbm, hbm, hbm],
        out_specs=(hbm, hbm),
        scratch_shapes=[blocks] * 3 + [blocks, packed, blocks] * 2 + [pairs] * 3 + [blocks] * 5 + [pairs]
        + [pltpu.VMEM((8 * BPD, 2 * B), F32), lines, pltpu.VMEM((4, BPD, B), F32), lines, lines]
        + [halo] * 3 + [pltpu.VMEM((ITERS, 2, 8, B), F32), pltpu.VMEM((ITERS, 4, 8, B), F32)]
        + [(pltpu.VMEM((BPD // CHUNKS, B, B), F32),) * CHUNKS] * 2
        + [dma((6,)), dma((3, N)), dma((3, N)), dma((ITERS, 2)), dma((ITERS, 2)), dma((ITERS, 4)), dma((ITERS, 4)), dma((CHUNKS, 2))],
        compiler_params=pltpu.CompilerParams(
            collective_id=0, has_side_effects=True, vmem_limit_bytes=60 * 1024 * 1024
        ),
    )(table, lengths, right_side, diag_blocks, lower_blocks)


def solution(mesh):
    blocks = P(("grp", "row"), None, None)
    return jax.shard_map(
        body,
        mesh=mesh,
        in_specs=(P("grp"), P("grp"), blocks, blocks, blocks),
        out_specs=(blocks, blocks),
        check_vma=False,
    )
```

time: 418 us -> 195 us (0.47); the launches traced: 411 us -> 195 us
  Pallas kernels: 0 us -> 187 us
  waiting for transfers between devices: 136 us -> 0 us
  blocking collectives: 127 us -> 0 us
  matrix products: 47.6 us -> 0 us
  starting transfers between devices: 34.4 us -> 0 us
  other arithmetic: 32.6 us -> 1.52 us
  local copies, waits for them, and re-layouts: 32.6 us -> 5.37 us
    pallas_call x0 -> x1, Pallas kernels: none -> 187 us  [body(): pl.pallas_call(kernel, out_shape=(field, field), in_specs=[smem, smem, hb...]
    all_to_all x1 -> x0, waiting for transfers between devices: 127 us -> none  [side_by_side(): lax.all_to_all(both, axis, split_axis=split_dim, concat_axis=concat_dim,...]
    all_to_all x8 -> x0, blocking collectives: 127 us -> none  [the longest x4 74.5 us: summed_on_arrival(): tiles = lax.all_to_all(cut_along(x, dim, count), axis, 0, 0, tiled=True)]
    dot_general x27 -> x0, matrix products: 47.6 us -> none  [the longest x4 17.6 us: operate(): jnp.einsum('jab,jbk->jak', coupling_low, shifted_down, precision=HIGHEST)]
    gather x10 -> x0, local copies, waits for them, and re-layouts: 24.5 us -> none  [the longest x4 7.28 us: body(): jnp.take_along_axis(slot_table, jnp.argsort(slot_table // per_dev, axis=1...]
    ppermute x8 -> x0, starting transfers between devices: 22.7 us -> none  [passed_along(): return lax.ppermute(x, axis, pairs)]
    sub x7 -> x0, other arithmetic: 21.2 us -> none  [the longest x4 21.2 us: body(): residual = residual - spread(step_size) * along_image]
    all_to_all x1 -> x0, starting transfers between devices: 11.7 us -> none  [side_by_side(): lax.all_to_all(both, axis, split_axis=split_dim, concat_axis=concat_dim,...]
  transfers between devices with their start and end apart: 9 -> 0, of which waited for: 5 -> 0; matrix products, arithmetic and copies ran while one was open for 7% -> 0% of each run, Pallas kernels for 0% -> 0%
where the time goes in v1:
time: 195 us
  Pallas kernels  187 us (96%)
  local copies, waits for them, and re-layouts  5.37 us (3%)
    pallas_call x1, Pallas kernels, body(): pl.pallas_call(kernel, out_shape=(field, field), in_specs=[smem, smem, hb...  187 us
    unnamed x4, local copies, waits for them, and re-layouts  4.61 us

profile of v1, /device:TPU:4, one launch (start us, length us, event | category | flops | bytes accessed | tf_op | source)
XLA Modules:
  0.0 194.9 jit_solution(4281493871359019627)
XLA Ops:
  0.6 0.8 reshape.57
  1.4 0.1 select_reduce_fusion.1
  1.5 0.1 select_reduce_fusion.2
  1.6 0.7 select_reduce_fusion
  2.3 0.6 pad_add_fusion.table
  2.9 187.3 %shard_map.68 = (f32[32,128,128]{2,1,0:T(8,128)}, f32[32,128,128]{2,1,0:T(8,128)}) custom-call(s32[96]{0:T(128)} %pad_add_fusion.table, s32[64]{0:T(128)} %lengths.1, f32[32,128,128]{2,1,0:T(8,128)} %rhs_hbm.1, f32[32,128,128]{2,1,0:T(8,128)} %diag_hbm.1, f32[32,128,128]{2,1,0:T(8,128)} %low_hbm.1), custom_call_target="tpu_custom_call" | custom-call | tf_op jit(solution)/shard_map/pallas_call | solution.py:368
  190.3 0.0 copy-start
  190.3 3.3 %copy.9 = f32[32,128,128]{2,1,0:T(8,128)} copy(f32[32,128,128]{2,1,0:T(8,128)} %get-tuple-element.8) | data formatting | bytes 4194304
  193.6 0.0 copy-done
  193.6 1.3 copy.10
  (1 shorter events, 0.0 us)
Async XLA Ops:
  190.3 3.3 %copy-start = (f32[32,128,128]{2,1,0:T(8,128)S(1)}, f32[32,128,128]{2,1,0:T(8,128)}, u32[]{:S(2)}) copy-start(f32[32,128,128]{2,1,0:T(8,128)} %get-tuple-element.9) | copy-start | bytes 6291460

commit v2 on v1

--- a/solution.py
+++ b/solution.py
@@ -62,7 +62,7 @@
     table, lengths, rhs_hbm, diag_hbm, low_hbm, x_hbm, r_hbm,
     st_f, st_d, st_l, sd_f, sd_d, sd_l, rc_f, rc_d, rc_l,
     w_d, w_t, w_l, x, r, p, s, im, rw, ss_rows, keep, near, alpha, beta,
-    halo_p, halo_t, turned, part, parts, x_out, r_out,
+    ends_f, ends_im, ends_r, ends_s, ends_rw, first_l, next_l, w_n, part, parts, x_out, r_out,
     in_sem, a2a_send, a2a_recv, halo_send, halo_recv, part_send, part_recv, out_sem,
 ):
     me = lax.axis_index("row")
@@ -88,17 +88,19 @@
         pl.semaphore_signal(barrier, 1, device_id={"row": away(i, 1)}, device_id_type=MESH)
         return carry
 
+    cut = ((), (pl.ds(0, H + 1),), ())
+
     def sent(phase, i, src, dst):
         t = away(i, 1)
         return pltpu.make_async_remote_copy(
-            src.at[t], dst.at[me], a2a_send.at[phase, i], a2a_recv.at[phase, i],
+            src.at[(t,) + cut[phase]], dst.at[(me,) + cut[phase]], a2a_send.at[phase, i], a2a_recv.at[phase, i],
             device_id={"row": t}, device_id_type=MESH,
         )
 
     def arriving(phase, i, src, dst):
         d = away(i, -1)
         return pltpu.make_async_remote_copy(
-            src.at[d], dst.at[d], a2a_send.at[phase, i], a2a_recv.at[phase, i],
+            src.at[(d,) + cut[phase]], dst.at[(d,) + cut[phase]], a2a_send.at[phase, i], a2a_recv.at[phase, i],
             device_id={"row": d}, device_id_type=MESH,
         )
 
@@ -186,6 +188,14 @@
         near[k] = jnp.broadcast_to(same[:, k : k + 1], (BPD, B))
     same_here = jnp.where(jnp.concatenate([seg, seg], axis=1) == seg_eighths, 1.0, 0.0).astype(F32)
 
+    def shift(by):
+        return (me + by + N) % N
+
+    def remote(src, dst, send, recv, by):
+        return pltpu.make_async_remote_copy(
+            src, dst, send, recv, device_id={"row": shift(by)}, device_id_type=MESH
+        )
+
     receive_all(0)
 
     def open_l(d, carry):
@@ -195,6 +205,9 @@
         return carry
 
     lax.fori_loop(0, N, open_l, 0)
+    first_l[...] = rc_l[src_of(0)]
+    couple = remote(first_l, next_l, halo_send.at[ITERS, 0], halo_recv.at[ITERS, 0], -1)
+    couple.start()
     receive_all(1)
 
     def open_d(d, carry):
@@ -202,6 +215,8 @@
         return carry
 
     lax.fori_loop(0, N, open_d, 0)
+    couple.wait()
+    w_n[...] = side(next_l[...].T)
     receive_all(2)
 
     def settle(l, carry):
@@ -212,50 +227,50 @@
 
     lax.fori_loop(0, BPD, settle, 0)
 
-    def shift(by):
-        return (me + by + N) % N
-
-    def remote(src, dst, send, recv, by):
-        return pltpu.make_async_remote_copy(
-            src, dst, send, recv, device_id={"row": shift(by)}, device_id_type=MESH
-        )
+    def swap(field, into, it):
+        return [
+            remote(field.at[row], into.at[k], halo_send.at[it, k], halo_recv.at[it, k], by)
+            for k, (row, by) in enumerate(((BPD - 1, 1), (0, -1)))
+        ]
+
+    def joined(k, value):
+        flag = near[0][0:1] if k == 0 else near[2][BPD - 1 : BPD]
+        return jnp.where(flag > 0.0, value, 0.0)
+
+    swap_f = swap(r, ends_f, ITERS - 1)
+    for copy in swap_f:
+        copy.start()
 
     def multiply(it):
-        down = remote(r.at[BPD - 1], halo_p.at[it], halo_send.at[it, 0], halo_recv.at[it, 0], 1)
-        up = remote(turned.at[it], halo_t.at[it], halo_send.at[it, 1], halo_recv.at[it, 1], -1)
-        down.start()
-
-        def products(j, last=False):
+        def products(j, kinds):
             here = src_of(j)
-            mats = [w_t[here], w_d[here]]
-            if not last:
-                mats.append(w_l[src_of(j + 1)])
-            out = times(jnp.concatenate(mats, axis=0), rw[j])
-            return [out[k * B : (k + 1) * B] for k in range(len(mats))]
-
-        t, c, b = products(0)
-        turned[it] = t
-        up.start()
+            mats = {"t": lambda: w_t[here], "d": lambda: w_d[here], "l": lambda: w_l[src_of(j + 1)]}
+            out = times(jnp.concatenate([mats[kind]() for kind in kinds], axis=0), rw[j])
+            return [out[k * B : (k + 1) * B] for k in range(len(kinds))]
+
+        c, b = products(0, "dl")
         im[0] = c
         im[1] = b
 
         def step(j, carry):
-            t, c, b = products(j)
+            t, c, b = products(j, "tdl")
             im[j - 1] = im[j - 1] + t
             im[j] = im[j] + c
             im[j + 1] = b
             return carry
 
         lax.fori_loop(1, BPD - 1, step, 0)
-        t, c = products(BPD - 1, last=True)
+        t, c = products(BPD - 1, "td")
         im[BPD - 2] = im[BPD - 2] + t
-        im[BPD - 1] = im[BPD - 1] + c
-        down.wait_recv()
-        im[0] = im[0] + times(w_l[src_of(0)], side(halo_p[it]))
-        up.wait_recv()
-        im[BPD - 1] = im[BPD - 1] + halo_t[it]
-        down.wait_send()
-        up.wait_send()
+        if it == 0:
+            for copy in swap_f:
+                copy.wait()
+            for k in range(2):
+                v = joined(k, ends_f[k])
+                ends_r[k] = v
+                ends_rw[k] = side(v)
+        im[0] = im[0] + times(w_l[src_of(0)], ends_rw[0])
+        im[BPD - 1] = im[BPD - 1] + (c + times(w_n[...], ends_rw[1]))
 
     def two_sums(it):
         def row_sums(l, carry):
@@ -287,7 +302,12 @@
 
     for it in range(ITERS):
         multiply(it)
+        swap_im = swap(im, ends_im.at[it], it) if it + 1 < ITERS else []
+        for copy in swap_im:
+            copy.start()
         norm, product = two_sums(it)
+        for copy in swap_im:
+            copy.wait()
         if it == 0:
             step_size = norm / product
         else:
@@ -317,6 +337,14 @@
 
         if it + 1 < ITERS:
             lax.fori_loop(0, BPD, update, 0)
+            for k, row in enumerate((0, BPD - 1)):
+                along = joined(k, ends_im[it, k])
+                if it > 0:
+                    along = along + beta[row : row + 1] * ends_s[k]
+                res = ends_r[k] - alpha[row : row + 1] * along
+                ends_s[k] = along
+                ends_r[k] = res
+                ends_rw[k] = side(res)
 
     outs = []
     span = BPD // CHUNKS
@@ -363,7 +391,8 @@
     packed = pltpu.VMEM((BPD, DROWS, B), F32)
     pairs = pltpu.VMEM((BPD, B, 2 * B), BF16)
     lines = pltpu.VMEM((BPD, B), F32)
-    halo = pltpu.VMEM((ITERS, B, B), F32)
+    pair = pltpu.VMEM((2, B, B), F32)
+    block = pltpu.VMEM((B, B), F32)
     dma = pltpu.SemaphoreType.DMA
     return pl.pallas_call(
         kernel,
@@ -372,9 +401,10 @@
         out_specs=(hbm, hbm),
         scratch_shapes=[blocks] * 3 + [blocks, packed, blocks] * 2 + [pairs] * 3 + [blocks] * 5 + [pairs]
         + [pltpu.VMEM((8 * BPD, 2 * B), F32), lines, pltpu.VMEM((4, BPD, B), F32), lines, lines]
-        + [halo] * 3 + [pltpu.VMEM((ITERS, 2, 8, B), F32), pltpu.VMEM((ITERS, 4, 8, B), F32)]
+        + [pair, pltpu.VMEM((ITERS - 1, 2, B, B), F32), pair, pair, pltpu.VMEM((2, B, 2 * B), BF16), block, block]
+        + [pltpu.VMEM((B, 2 * B), BF16), pltpu.VMEM((ITERS, 2, 8, B), F32), pltpu.VMEM((ITERS, 4, 8, B), F32)]
         + [(pltpu.VMEM((BPD // CHUNKS, B, B), F32),) * CHUNKS] * 2
-        + [dma((6,)), dma((3, N)), dma((3, N)), dma((ITERS, 2)), dma((ITERS, 2)), dma((ITERS, 4)), dma((ITERS, 4)), dma((CHUNKS, 2))],
+        + [dma((6,)), dma((3, N)), dma((3, N)), dma((ITERS + 1, 2)), dma((ITERS + 1, 2)), dma((ITERS, 4)), dma((ITERS, 4)), dma((CHUNKS, 2))],
         compiler_params=pltpu.CompilerParams(
             collective_id=0, has_side_effects=True, vmem_limit_bytes=60 * 1024 * 1024
         ),

time: 195 us -> 193 us (0.990)
  Pallas kernels: 187 us -> 185 us
    pallas_call x1, Pallas kernels: 187 us -> 185 us  [body(): pl.pallas_call(kernel, out_shape=(field, field), in_specs=[smem, smem, hb...]
where the time goes in v2:
time: 193 us
  Pallas kernels  185 us (96%)
  local copies, waits for them, and re-layouts  5.37 us (3%)
    pallas_call x1, Pallas kernels, body(): pl.pallas_call(kernel, out_shape=(field, field), in_specs=[smem, smem, hb...  185 us
    unnamed x4, local copies, waits for them, and re-layouts  4.61 us

profile of v2, /device:TPU:4, one launch (start us, length us, event | category | flops | bytes accessed | tf_op | source)
XLA Modules:
  0.0 192.8 jit_solution(58869660466364332)
XLA Ops:
  0.6 0.8 reshape.57
  1.4 0.1 select_reduce_fusion.1
  1.5 0.1 select_reduce_fusion.2
  1.6 0.7 select_reduce_fusion
  2.3 0.6 pad_add_fusion.table
  2.9 185.2 %shard_map.68 = (f32[32,128,128]{2,1,0:T(8,128)}, f32[32,128,128]{2,1,0:T(8,128)}) custom-call(s32[96]{0:T(128)} %pad_add_fusion.table, s32[64]{0:T(128)} %lengths.1, f32[32,128,128]{2,1,0:T(8,128)} %rhs_hbm.1, f32[32,128,128]{2,1,0:T(8,128)} %diag_hbm.1, f32[32,128,128]{2,1,0:T(8,128)} %low_hbm.1), custom_call_target="tpu_custom_call" | custom-call | tf_op jit(solution)/shard_map/pallas_call | solution.py:397
  188.1 0.0 copy-start
  188.1 3.3 %copy.9 = f32[32,128,128]{2,1,0:T(8,128)} copy(f32[32,128,128]{2,1,0:T(8,128)} %get-tuple-element.8) | data formatting | bytes 4194304
  191.4 0.0 copy-done
  191.4 1.3 copy.10
  (1 shorter events, 0.0 us)
Async XLA Ops:
  188.1 3.3 %copy-start = (f32[32,128,128]{2,1,0:T(8,128)S(1)}, f32[32,128,128]{2,1,0:T(8,128)}, u32[]{:S(2)}) copy-start(f32[32,128,128]{2,1,0:T(8,128)} %get-tuple-element.9) | copy-start | bytes 6291460
